TPU v7x, 256 devices: a whole 4x4x8 slice. The times are simulated.
256 devices in a mesh: space: 16 (over z, x_hi), mrow: 4 (over y), mcol: 4 (over x_lo, core).
Axes of the slice: x: 4 (x_hi: 2, x_lo: 2; x = x_hi * 2 + x_lo), y: 4, z: 8, core: 2. Of those that a mesh axis runs over, the one named last changes fastest.
Arguments:
- deviation: bfloat16 [512, 48, 8192], P('space', None, ('mcol', 'mrow'))
- courant: float32 [2, 8192], P(None, ('mcol', 'mrow')), may hold values from -0.95 to 0.95
- collide: bfloat16 [8192, 8192], P('mrow', ('mcol', 'space'))
- hole_cells: int32 [6144], P('space'), may hold values from -1 to 1535, as said below
- hole_wall: int32 [6144], P('space'), may hold values from 0 to 3
- specular: int32 [4, 8192], replicated, may hold values from 0 to 8191, as said below
- specularity: float32 [4], replicated, may hold values from 0.2 to 0.8
Outputs:
- updated: bfloat16 [512, 48, 8192], P('space', None, ('mrow', 'mcol'))
Inputs may be any that keep to these rules, and one draw needn't show every extreme that they name: `hole_cells`: within one tile the used slots come first and name distinct cells; every tile has at least 96 used slots, some tile has all 384 slots used and some tile has an empty slot. Each row specular[w] is a permutation of the modes; for an outgoing mode i of aligned block e = i // 512, its incoming mode j lies, within j's own aligned block of 512 modes, in the sub-block of 32 modes numbered e, that is (j % 512) // 32 == e.
All inputs are finite; a program needn't handle non-finite values.
Results may differ from a plain program's by a relative error of at most 0.005.
Values may be sent and summed in bfloat16 or wider, within the bound.
A program may use at most 128 MiB of HBM per device.

v0:
```python
import jax
import jax.numpy as jnp
from jax import lax
from jax.sharding import PartitionSpec as P


def extended(x, sides, width):
    for axis, dim in sides:
        size, length = (lax.axis_size(axis), x.shape[dim])
        up = [(i, (i + 1) % size) for i in range(size - 1)]
        down = [(j, i) for i, j in up]
        last = lax.slice_in_dim(x, length - width, length, axis=dim)
        first = lax.slice_in_dim(x, 0, width, axis=dim)
        before = lax.ppermute(last, axis, up)
        after = lax.ppermute(first, axis, down)
        x = jnp.concatenate([before, x, after], axis=dim)
    return x


def upwind(padded, courant):
    field = padded.astype(jnp.float32)
    reach_x = jnp.abs(courant[0])
    reach_y = jnp.abs(courant[1])
    center = field[1:-1]
    upwind_x = jnp.where(courant[0] > 0, field[:-2], field[2:])
    upwind_y = jnp.where(courant[1] > 0, jnp.roll(center, 1, axis=1), jnp.roll(center, -1, axis=1))
    upwind_xy = jnp.where(
        courant[1] > 0, jnp.roll(upwind_x, 1, axis=1), jnp.roll(upwind_x, -1, axis=1)
    )
    result = (1.0 - reach_x) * (1.0 - reach_y) * center + reach_x * (1.0 - reach_y) * upwind_x
    result = result + (1.0 - reach_x) * reach_y * upwind_y + reach_x * reach_y * upwind_xy
    return result.astype(jnp.bfloat16)


def mirror_values(source_rows, wall_tables, one_hot):
    flipped = source_rows.T
    picked = flipped[wall_tables].astype(jnp.float32)
    weights = one_hot.T.astype(jnp.float32)
    chosen = jnp.sum(weights[:, None, :] * picked, axis=0)
    return chosen.T


def reemit(full_rows, wall_tables, one_hot, share):
    mirrored = mirror_values(full_rows, wall_tables, one_hot)
    diffuse = jnp.sum(full_rows.astype(jnp.float32), axis=1) / full_rows.shape[1]
    return (share[:, None] * mirrored + (1.0 - share)[:, None] * diffuse[:, None]).astype(
        jnp.bfloat16
    )


def on_device(deviation, courant, collide, hole_cells, hole_wall, specular, specularity):
    padded = extended(deviation, (("space", 0),), 1)
    read = upwind(padded, courant)
    width_x, width_y, block_len = read.shape
    cell_count = width_x * width_y
    row_groups = lax.axis_size("mrow")
    col_groups = lax.axis_size("mcol")
    is_live = hole_cells >= 0
    safe_ids = jnp.where(is_live, hole_cells, 0)
    target_ids = jnp.where(is_live, hole_cells, cell_count)
    wall_count = specular.shape[0]
    one_hot = hole_wall[:, None] == jnp.arange(wall_count, dtype=jnp.int32)[None, :]
    share = jnp.dot(one_hot.astype(jnp.float32), specularity, precision=lax.Precision.HIGHEST)
    flat_cells = read.reshape(cell_count, block_len)
    start = (lax.axis_index("mcol") * row_groups + lax.axis_index("mrow")) * block_len
    own_table = lax.dynamic_slice_in_dim(specular, start, block_len, 1)
    block_ids = own_table // block_len
    positions = (
        block_ids % row_groups * col_groups + block_ids // row_groups
    ) * block_len + own_table % block_len
    full_rows = lax.all_gather(flat_cells[safe_ids], ("mrow", "mcol"), axis=1, tiled=True)
    emitted = reemit(full_rows, positions, one_hot, share)
    flat_cells = flat_cells.at[target_ids].set(emitted, mode="drop")
    columns = lax.all_gather(
        flat_cells.reshape(width_x, width_y, block_len), "mrow", axis=2, tiled=True
    )
    column_flat = columns.reshape(cell_count, columns.shape[2])
    partial_sums = lax.dot_general(
        column_flat,
        lax.all_gather(collide, "space", axis=1, tiled=True),
        (((1,), (1,)), ((), ())),
        preferred_element_type=jnp.float32,
    )
    summed = lax.psum_scatter(partial_sums, "mcol", scatter_dimension=1, tiled=True)
    return summed.astype(jnp.bfloat16).reshape(width_x, width_y, summed.shape[1])


def solution(mesh):
    in_specs = (
        P("space", None, ("mcol", "mrow")),
        P(None, ("mcol", "mrow")),
        P("mrow", ("mcol", "space")),
        P("space"),
        P("space"),
        P(),
        P(),
    )
    out_specs = P("space", None, ("mrow", "mcol"))
    return jax.shard_map(
        on_device, mesh=mesh, in_specs=in_specs, out_specs=out_specs, check_vma=False
    )
```

profile of v0, /device:TPU:1, one launch (start us, length us, event | category | flops | bytes accessed | tf_op | source)
XLA Modules:
  0.0 448.5 jit_solution(13947178258278800401)
XLA Ops:
  6.5 0.8 fusion.22
  7.4 5.5 %collective-permute-start = (bf16[1,48,512]{2,1,0:T(8,128)(2,1)S(1)}, bf16[1,48,512]{2,1,0:T(8,128)(2,1)S(1)}, u32[]{:S(2)}, u32[]{:S(2)}) collective-permute-start(bf16[1,48,512]{2,1,0:T(8,128)(2,1)S(1)} %get-tuple-element.15), channel_id=1, source_target_pairs={{0,16},{16,32},{32,48},{48,64},{64,80},{80,96},{96,112},{112,128},... | collective-permute-start | bytes 147464 | tf_op jit(solution)/shard_map/ppermute | solution.py:14
  12.8 1.3 collective-permute-start.1
  14.1 0.8 compare_reduce_fusion
  14.9 0.8 slice_abs_fusion
  16.4 2.8 collective-permute-done.1
  19.2 1.7 maximum_convert_fusion
  21.5 4.9 %fusion.19 = (f32[32,47,512]{2,1,0:T(8,128)}, f32[32,47,512]{2,1,0:T(8,128)}, f32[32,47,512]{2,1,0:T(8,128)}, f32[32,47,512]{2,1,0:T(8,128)}) fusion(f32[34,48,512]{2,1,0:T(8,128)S(1)} %maximum_convert_fusion, f32[32,48,512]{2,1,0:T(8,128)S(1)} %slice_select_fusion), kind=kLoop, calls=%fused_computation.62 | loop fusion | bytes 24641536 | tf_op jit(solution)/shard_map/jit(_roll_static)/slice | solution.py:26
  26.5 1.1 maximum_convert_fusion.1
  27.6 6.2 %fusion.3 = bf16[32,48,512]{2,1,0:T(8,128)(2,1)S(1)} fusion(f32[34,48,512]{2,1,0:T(8,128)S(1)} %maximum_convert_fusion, f32[32,47,512]{2,1,0:T(8,128)} %get-tuple-element.8, f32[32,1,512]{2,1,0:T(1,128)S(1)} %get-tuple-element.14, f32[32,1,512]{2,1,0:T(1,128)S(1)} %get-tuple-element.13, f32[32,47,512]{2,1,0:T(8,128)} %get-tuple-element.7, ...), kind=kLoop, calls=%fused_computation.9 | loop fusion | flops 11796480 | bytes 23602176 | tf_op jit(solution)/shard_map/convert_element_type | solution.py:32
  33.9 2.6 gather_fusion
  36.5 0.7 all-gather.7.cloned.1.call-update
  37.3 0.7 fusion.16
  38.4 48.1 %all-gather.9.cloned.1.call-done = bf16[384,8192]{1,0:T(8,128)(2,1)} async-done(((bf16[384,512]{1,0:T(8,128)(2,1)}), bf16[384,8192]{1,0:T(8,128)(2,1)}) %all-gather.9.cloned.1.call-update) | async-done | bytes 6291472 | tf_op jit(solution)/shard_map/all_gather | solution.py:71
  86.5 8.7 %copy.9 = bf16[8192,384]{1,0:T(8,128)(2,1)} copy(bf16[8192,384]{0,1:T(8,128)(2,1)} %bitcast.22) | data formatting | bytes 12582912 | tf_op jit(solution)/shard_map/transpose | solution.py:36
  95.1 10.8 %gather_fusion.1 = bf16[2048,384]{1,0:T(8,128)(2,1)S(1)} fusion(bf16[8192,384]{1,0:T(8,128)(2,1)} %copy.9, s32[2048]{0:T(1024)S(1)} %broadcast_clamp_fusion), kind=kCustom, calls=%fused_computation.1 | custom fusion | bytes 3153920 | tf_op jit(solution)/shard_map/gather | solution.py:37
  106.3 3.7 convert_reduce_fusion
  110.3 2.8 scatter_fusion
  113.1 1.1 copy-done.2
  114.5 118.4 %all-gather.7.cloned.1.call-done = bf16[2048,2048]{1,0:T(8,128)(2,1)} async-done(((bf16[2048,128]{1,0:T(8,128)(2,1)}), bf16[2048,2048]{1,0:T(8,128)(2,1)}) %all-gather.7.cloned.1.call-update) | async-done | bytes 8388624 | tf_op jit(solution)/shard_map/all_gather | solution.py:80
  232.9 69.9 %all-gather.5.cloned.1.call-done = bf16[32,48,2048]{2,1,0:T(8,128)(2,1)} async-done(((bf16[32,48,512]{2,1,0:T(8,128)(2,1)}), bf16[32,48,2048]{2,1,0:T(8,128)(2,1)}) %all-gather.5.cloned.1.call-update) | async-done | bytes 6291472 | tf_op jit(solution)/shard_map/all_gather | solution.py:74
  302.9 19.0 %fusion.23 = f32[1536,2048]{1,0:T(8,128)} fusion(bf16[1536,2048]{1,0:T(8,128)(2,1)} %bitcast.27, bf16[2048,2048]{1,0:T(8,128)(2,1)} %all-gather.7.cloned.1.call-done), kind=kOutput, calls=%fused_computation.66 | convolution fusion | flops 12884901888 | bytes 27262976 | tf_op jit(solution)/shard_map/dot_general | solution.py:78
  322.0 116.8 %reduce-scatter.2.cloned.1.call-done = f32[1536,512]{1,0:T(8,128)} async-done(((f32[1536,2048]{1,0:T(8,128)}), f32[1536,512]{1,0:T(8,128)}) %reduce-scatter.2.cloned.1.call-update) | async-done | bytes 3145744 | tf_op jit(solution)/shard_map/reduce_scatter | solution.py:84
  438.7 3.2 convert_element_type.36
  (28 shorter events, 2.7 us)
Async XLA Ops:
  6.5 31.5 %copy-start = (f32[4]{0:T(128)S(1)}, f32[4]{0:T(128)}, u32[]{:S(2)}) copy-start(f32[4]{0:T(128)} %param.13) | copy-start | bytes 52
  6.5 79.9 %all-gather.9.cloned.1.call-start = ((), (), s32[]{:S(2)}) async-start(), calls=%async_computation.4 | async-start | bytes 6684672 | tf_op jit(solution)/shard_map/all_gather | solution.py:71
  7.4 9.0 %collective-permute-start = (bf16[1,48,512]{2,1,0:T(8,128)(2,1)S(1)}, bf16[1,48,512]{2,1,0:T(8,128)(2,1)S(1)}, u32[]{:S(2)}, u32[]{:S(2)}) collective-permute-start(bf16[1,48,512]{2,1,0:T(8,128)(2,1)S(1)} %get-tuple-element.15), channel_id=1, source_target_pairs={{0,16},{16,32},{32,48},{48,64},{64,80},{80,96},{96,112},{112,128},... | collective-permute-start | bytes 147464 | tf_op jit(solution)/shard_map/ppermute | solution.py:14
  12.8 6.3 %collective-permute-start.1 = (bf16[1,48,512]{2,1,0:T(8,128)(2,1)S(1)}, bf16[1,48,512]{2,1,0:T(8,128)(2,1)S(1)}, u32[]{:S(2)}, u32[]{:S(2)}) collective-permute-start(bf16[1,48,512]{2,1,0:T(8,128)(2,1)S(1)} %get-tuple-element.16), channel_id=1, source_target_pairs={{16,0},{32,16},{48,32},{64,48},{80,64},{96,80},{112,96},{128,112},... | collective-permute-start | bytes 147464 | tf_op jit(solution)/shard_map/ppermute | solution.py:15
  33.8 4.2 copy-start.3
  36.5 196.5 %all-gather.7.cloned.1.call-start = ((), (), s32[]{:S(2)}) async-start(), calls=%async_computation.2 | async-start | bytes 8912896 | tf_op jit(solution)/shard_map/all_gather | solution.py:80
  37.2 265.7 %all-gather.5.cloned.1.call-start = ((), (), s32[]{:S(2)}) async-start(), calls=%async_computation.1 | async-start | bytes 7864320 | tf_op jit(solution)/shard_map/all_gather | solution.py:74
  113.1 1.1 copy-start.2
  114.3 324.4 %reduce-scatter.2.cloned.1.call-start = ((), (), s32[]{:S(2)}) async-start(), calls=%async_computation.3 | async-start | bytes 15728640 | tf_op jit(solution)/shard_map/reduce_scatter | solution.py:84
  321.9 120.0 %copy-start.1 = (f32[4]{0:T(128)S(1)}, f32[4]{0:T(128)}, u32[]{:S(2)}) copy-start(f32[4]{0:T(128)} %param.13) | copy-start | bytes 52
Sparse Core Ops, SparseCore 0:
  36.6 49.8 all-gather.8
  88.9 143.9 all-gather.6
  234.8 68.0 all-gather.4
  322.1 116.6 reduce-scatter.1
where the time goes:
time: 449 us; the launch traced here: 448 us
  waiting for transfers between devices  357 us (80%)
  local copies, waits for them, and re-layouts  32.1 us (7%)
  other arithmetic  20 us (4%)
  matrix products  19.3 us (4%)
  between operations  13.3 us (3%)
  starting transfers between devices  7.05 us (2%)
    all_gather x1, waiting for transfers between devices, on_device(): lax.all_gather(collide, 'space', axis=1, tiled=True)  118 us
    reduce_scatter x1, waiting for transfers between devices, on_device(): lax.psum_scatter(partial_sums, 'mcol', scatter_dimension=1, tiled=True)  117 us
    all_gather x1, waiting for transfers between devices, on_device(): lax.all_gather(flat_cells.reshape(width_x, width_y, block_len), 'mrow', a...  69.9 us
    all_gather x1, waiting for transfers between devices, on_device(): lax.all_gather(flat_cells[safe_ids], ('mrow', 'mcol'), axis=1, tiled=True)  48.1 us
    dot_general x1, matrix products, on_device(): lax.dot_general(column_flat, lax.all_gather(collide, 'space', axis=1, til...  19 us
    gather x1, local copies, waits for them, and re-layouts, mirror_values(): picked = flipped[wall_tables].astype(jnp.float32)  10.8 us
  transfers between devices with their start and end apart: 6, of which 5 were waited for; matrix products, arithmetic and copies ran while one was open for 7% of the time, Pallas kernels for 0%

commit v1 on v0

--- a/solution.py
+++ b/solution.py
@@ -1,7 +1,18 @@
+import functools
 import jax
 import jax.numpy as jnp
 from jax import lax
 from jax.sharding import PartitionSpec as P
+
+
+def edit_rails(point, mesh_name, array_dim):
+    a_next = tuple((point for _ in range(lax.axis_size(mesh_name))))
+    placed = jnp.stack(a_next)
+    latest = lax.all_to_all(placed, axis_name=mesh_name, split_axis=0, concat_axis=0)
+    return jnp.concatenate(latest, axis=array_dim)
+
+
+finish_the_shards = functools.partial(edit_rails, mesh_name="mrow", array_dim=2)
 
 
 def extended(x, sides, width):
@@ -71,9 +82,7 @@
     full_rows = lax.all_gather(flat_cells[safe_ids], ("mrow", "mcol"), axis=1, tiled=True)
     emitted = reemit(full_rows, positions, one_hot, share)
     flat_cells = flat_cells.at[target_ids].set(emitted, mode="drop")
-    columns = lax.all_gather(
-        flat_cells.reshape(width_x, width_y, block_len), "mrow", axis=2, tiled=True
-    )
+    columns = finish_the_shards(flat_cells.reshape(width_x, width_y, block_len))
     column_flat = columns.reshape(cell_count, columns.shape[2])
     partial_sums = lax.dot_general(
         column_flat,

time: 449 us -> 379 us (0.84)
  waiting for transfers between devices: 357 us -> 196 us
  blocking collectives: 0 us -> 74.3 us
  local copies, waits for them, and re-layouts: 32.1 us -> 48.3 us
    all_gather x1, waiting for transfers between devices: 118 us -> 28.3 us  [on_device(): lax.all_gather(collide, 'space', axis=1, tiled=True)]
    all_to_all x0 -> x1, blocking collectives: none -> 74.3 us  [edit_rails(): lax.all_to_all(placed, axis_name=mesh_name, split_axis=0, concat_axis=0)]
    all_gather x1 -> x0, waiting for transfers between devices: 69.9 us -> none  [on_device(): lax.all_gather(flat_cells.reshape(width_x, width_y, block_len), 'mrow', a...]
    reshape x0 -> x1, local copies, waits for them, and re-layouts: none -> 8.47 us  [edit_rails(): return jnp.concatenate(latest, axis=array_dim)]
    unnamed x9 -> x8, local copies, waits for them, and re-layouts: 1.16 us -> 8.14 us
  transfers between devices with their start and end apart: 6 -> 5, of which waited for: 5 -> 4; matrix products, arithmetic and copies ran while one was open for 7% -> 13% of each run, Pallas kernels for 0% -> 0%
where the time goes in v1:
time: 379 us; the launch traced here: 378 us
  waiting for transfers between devices  196 us (52%)
  blocking collectives  74.3 us (20%)
  local copies, waits for them, and re-layouts  48.3 us (13%)
  other arithmetic  20 us (5%)
  matrix products  19.3 us (5%)
  between operations  13.3 us (4%)
  starting transfers between devices  6.83 us (2%)
    reduce_scatter x1, waiting for transfers between devices, on_device(): lax.psum_scatter(partial_sums, 'mcol', scatter_dimension=1, tiled=True)  116 us
    all_to_all x1, blocking collectives, edit_rails(): lax.all_to_all(placed, axis_name=mesh_name, split_axis=0, concat_axis=0)  74.3 us
    all_gather x1, waiting for transfers between devices, on_device(): lax.all_gather(flat_cells[safe_ids], ('mrow', 'mcol'), axis=1, tiled=True)  48.1 us
    all_gather x1, waiting for transfers between devices, on_device(): lax.all_gather(collide, 'space', axis=1, tiled=True)  28.3 us
    dot_general x1, matrix products, on_device(): lax.dot_general(column_flat, lax.all_gather(collide, 'space', axis=1, til...  19 us
    gather x1, local copies, waits for them, and re-layouts, mirror_values(): picked = flipped[wall_tables].astype(jnp.float32)  10.8 us
    transpose x1, local copies, waits for them, and re-layouts, mirror_values(): flipped = source_rows.T  8.62 us
    reshape x1, local copies, waits for them, and re-layouts, edit_rails(): return jnp.concatenate(latest, axis=array_dim)  8.47 us
  transfers between devices with their start and end apart: 5, of which 4 were waited for; matrix products, arithmetic and copies ran while one was open for 13% of the time, Pallas kernels for 0%

profile of v1, /device:TPU:1, one launch (start us, length us, event | category | flops | bytes accessed | tf_op | source)
XLA Modules:
  0.0 377.8 jit_solution(4761398377191515757)
XLA Ops:
  6.5 0.8 fusion.22
  7.4 5.5 %collective-permute-start = (bf16[1,48,512]{2,1,0:T(8,128)(2,1)S(1)}, bf16[1,48,512]{2,1,0:T(8,128)(2,1)S(1)}, u32[]{:S(2)}, u32[]{:S(2)}) collective-permute-start(bf16[1,48,512]{2,1,0:T(8,128)(2,1)S(1)} %get-tuple-element.15), channel_id=1, source_target_pairs={{0,16},{16,32},{32,48},{48,64},{64,80},{80,96},{96,112},{112,128},... | collective-permute-start | bytes 147464 | tf_op jit(solution)/shard_map/ppermute | solution.py:25
  12.8 1.3 collective-permute-start.1
  14.1 0.8 compare_reduce_fusion
  14.9 0.8 slice_abs_fusion
  16.4 2.8 collective-permute-done.1
  19.2 1.7 maximum_convert_fusion
  21.5 4.9 %fusion.19 = (f32[32,47,512]{2,1,0:T(8,128)}, f32[32,47,512]{2,1,0:T(8,128)}, f32[32,47,512]{2,1,0:T(8,128)}, f32[32,47,512]{2,1,0:T(8,128)}) fusion(f32[34,48,512]{2,1,0:T(8,128)S(1)} %maximum_convert_fusion, f32[32,48,512]{2,1,0:T(8,128)S(1)} %slice_select_fusion), kind=kLoop, calls=%fused_computation.62 | loop fusion | bytes 24641536 | tf_op jit(solution)/shard_map/jit(_roll_static)/slice | solution.py:37
  26.5 1.1 maximum_convert_fusion.1
  27.6 6.2 %fusion.3 = bf16[32,48,512]{2,1,0:T(8,128)(2,1)S(1)} fusion(f32[34,48,512]{2,1,0:T(8,128)S(1)} %maximum_convert_fusion, f32[32,47,512]{2,1,0:T(8,128)} %get-tuple-element.8, f32[32,1,512]{2,1,0:T(1,128)S(1)} %get-tuple-element.14, f32[32,1,512]{2,1,0:T(1,128)S(1)} %get-tuple-element.13, f32[32,47,512]{2,1,0:T(8,128)} %get-tuple-element.7, ...), kind=kLoop, calls=%fused_computation.9 | loop fusion | flops 11796480 | bytes 23602176 | tf_op jit(solution)/shard_map/convert_element_type | solution.py:43
  33.8 2.6 gather_fusion
  38.4 48.1 %all-gather.6.cloned.1.call-done = bf16[384,8192]{1,0:T(8,128)(2,1)} async-done(((bf16[384,512]{1,0:T(8,128)(2,1)}), bf16[384,8192]{1,0:T(8,128)(2,1)}) %all-gather.6.cloned.1.call-update) | async-done | bytes 6291472 | tf_op jit(solution)/shard_map/all_gather | solution.py:82
  86.5 8.6 %copy.10 = bf16[8192,384]{1,0:T(8,128)(2,1)} copy(bf16[8192,384]{0,1:T(8,128)(2,1)} %bitcast.25) | data formatting | bytes 12582912 | tf_op jit(solution)/shard_map/transpose | solution.py:47
  95.1 10.8 %gather_fusion.1 = bf16[2048,384]{1,0:T(8,128)(2,1)S(1)} fusion(bf16[8192,384]{1,0:T(8,128)(2,1)} %copy.10, s32[2048]{0:T(1024)S(1)} %broadcast_clamp_fusion), kind=kCustom, calls=%fused_computation.1 | custom fusion | bytes 3153920 | tf_op jit(solution)/shard_map/gather | solution.py:48
  106.2 3.7 convert_reduce_fusion
  110.2 2.8 scatter_fusion
  113.1 0.8 stack.3
  113.8 74.3 %all_to_all.5 = bf16[4,32,48,512]{3,2,1,0:T(8,128)(2,1)S(1)} all-to-all(bf16[4,32,48,512]{3,2,1,0:T(8,128)(2,1)S(1)} %stack.3), channel_id=1, replica_groups=mesh['space'=16,'mrow'=4,'mcol'=4] {'mrow'}, dimensions={0} | all-to-all | bytes 12582912 | tf_op jit(solution)/shard_map/all_to_all | solution.py:11
  188.2 8.5 %copy.12 = bf16[32,48,4,512]{3,2,1,0:T(4,128)(2,1)} copy(bf16[32,48,4,512]{3,1,0,2:T(8,128)(2,1)S(1)} %bitcast.26) | data formatting | bytes 12582912 | tf_op jit(solution)/shard_map/reshape | solution.py:12
  196.6 8.1 %copy.14 = bf16[192,8,4,512]{3,1,2,0:T(8,128)(2,1)} copy(bf16[192,8,4,512]{3,2,1,0:T(4,128)(2,1)} %bitcast.27) | data formatting | bytes 12582912
  204.7 28.3 %all-gather.4.cloned.1.call-done = bf16[2048,2048]{1,0:T(8,128)(2,1)} async-done(((bf16[2048,128]{1,0:T(8,128)(2,1)}), bf16[2048,2048]{1,0:T(8,128)(2,1)}) %all-gather.4.cloned.1.call-update) | async-done | bytes 8388624 | tf_op jit(solution)/shard_map/all_gather | solution.py:89
  233.0 19.0 %fusion.23 = f32[1536,2048]{1,0:T(8,128)} fusion(bf16[1536,2048]{1,0:T(8,128)(2,1)} %bitcast.28, bf16[2048,2048]{1,0:T(8,128)(2,1)} %all-gather.4.cloned.1.call-done), kind=kOutput, calls=%fused_computation.66 | convolution fusion | flops 12884901888 | bytes 27262976 | tf_op jit(solution)/shard_map/dot_general | solution.py:87
  252.1 116.0 %reduce-scatter.2.cloned.1.call-done = f32[1536,512]{1,0:T(8,128)} async-done(((f32[1536,2048]{1,0:T(8,128)}), f32[1536,512]{1,0:T(8,128)}) %reduce-scatter.2.cloned.1.call-update) | async-done | bytes 3145744 | tf_op jit(solution)/shard_map/reduce_scatter | solution.py:93
  368.1 3.2 convert_element_type.36
  (27 shorter events, 3.9 us)
Async XLA Ops:
  6.5 31.5 %copy-start = (f32[4]{0:T(128)S(1)}, f32[4]{0:T(128)}, u32[]{:S(2)}) copy-start(f32[4]{0:T(128)} %param.13) | copy-start | bytes 52
  6.5 79.9 %all-gather.6.cloned.1.call-start = ((), (), s32[]{:S(2)}) async-start(), calls=%async_computation.4 | async-start | bytes 6684672 | tf_op jit(solution)/shard_map/all_gather | solution.py:82
  7.4 9.0 %collective-permute-start = (bf16[1,48,512]{2,1,0:T(8,128)(2,1)S(1)}, bf16[1,48,512]{2,1,0:T(8,128)(2,1)S(1)}, u32[]{:S(2)}, u32[]{:S(2)}) collective-permute-start(bf16[1,48,512]{2,1,0:T(8,128)(2,1)S(1)} %get-tuple-element.15), channel_id=1, source_target_pairs={{0,16},{16,32},{32,48},{48,64},{64,80},{80,96},{96,112},{112,128},... | collective-permute-start | bytes 147464 | tf_op jit(solution)/shard_map/ppermute | solution.py:25
  12.8 6.3 %collective-permute-start.1 = (bf16[1,48,512]{2,1,0:T(8,128)(2,1)S(1)}, bf16[1,48,512]{2,1,0:T(8,128)(2,1)S(1)}, u32[]{:S(2)}, u32[]{:S(2)}) collective-permute-start(bf16[1,48,512]{2,1,0:T(8,128)(2,1)S(1)} %get-tuple-element.16), channel_id=1, source_target_pairs={{16,0},{32,16},{48,32},{64,48},{80,64},{96,80},{112,96},{128,112},... | collective-permute-start | bytes 147464 | tf_op jit(solution)/shard_map/ppermute | solution.py:26
  33.8 4.2 %copy-start.2 = (s32[384]{0:T(512)S(1)}, s32[384]{0:T(512)}, u32[]{:S(2)}) copy-start(s32[384]{0:T(512)} %param.11) | copy-start | bytes 4612
  36.4 196.6 %all-gather.4.cloned.1.call-start = ((), (), s32[]{:S(2)}) async-start(), calls=%async_computation.2 | async-start | bytes 8912896 | tf_op jit(solution)/shard_map/all_gather | solution.py:89
  37.2 330.9 %reduce-scatter.2.cloned.1.call-start = ((), (), s32[]{:S(2)}) async-start(), calls=%async_computation.3 | async-start | bytes 15728640 | tf_op jit(solution)/shard_map/reduce_scatter | solution.py:93
  252.1 119.3 %copy-start.1 = (f32[4]{0:T(128)S(1)}, f32[4]{0:T(128)}, u32[]{:S(2)}) copy-start(f32[4]{0:T(128)} %param.13) | copy-start | bytes 52
Sparse Core Ops, SparseCore 0:
  36.6 49.8 all-gather.5
  88.9 144.0 all-gather.3
  252.2 115.8 reduce-scatter.1
